TPU v7x, 32 devices: a whole 2x2x4 slice. The times are simulated.
32 devices in a mesh: groups: 2 (over y), wave: 4 (over z), section: 4 (over x, core).
Axes of the slice: x: 2, y: 2, z: 4, core: 2. Of those that a mesh axis runs over, the one named last changes fastest.
Arguments:
- nominal_field: float32 [4, 2, 1024], P('wave'), may hold values from -6 to 6
- sensitivity: bfloat16 [4, 360, 2, 1024], P('wave'), may hold values from -0.3125 to 0.3125
- aberrations: bfloat16 [128, 360], P('groups'), parts along dimension 0, may hold values from -13 to 13
- jacobian: bfloat16 [4, 2, 1024, 8192], P('wave', None, None, 'section'), may hold values from -1 to 1
- tile_mask: int32 [4, 8], P('wave'), may hold values 0 or 1
- regul: float32 [8192], P('section'), may hold values from 0.05 to 0.5
- initial_commands: float32 [128, 8192], P('groups', 'section'), parts along dimension 0, may hold values from -3 to 3
Outputs:
- commands: float32 [128, 8192], P('groups', 'section'), parts along dimension 0
- dark_field: float32 [128, 4, 2, 1024], P('groups', 'wave'), parts along dimension 0
There are 2 independent parts, one for each index of `groups`. A program takes and returns all parts, laid end to end along the dimension named above; an argument that names none is the same for every part. Nothing has to cross between parts.
All inputs are finite; a program needn't handle non-finite values. No bound on the sum of `tile_mask` on one device may be relied on, other than what follows from the above.
Results may differ from a plain program's by a relative error of at most 0.035.
Values may be sent and summed in bfloat16 or wider, within the bound.
A program may use at most 64 MiB of HBM per device.

v0:
```python
import jax
import jax.numpy as jnp
from jax import lax
from jax.sharding import PartitionSpec as P

ITERS = 2
CG = 5


epsilon = 1e-06


def to_section_image(command_bf, jac_block):
    partial_value = lax.dot_general(
        command_bf, jac_block, (((1,), (1,)), ((), ())), preferred_element_type=jnp.float32
    )
    return lax.psum_scatter(
        partial_value.astype(jnp.bfloat16), "section", scatter_dimension=1, tiled=True
    ).astype(jnp.float32)


def back_of(masked_share, jac_block):
    masked_bf = lax.all_gather(masked_share, "section", axis=1, tiled=True)
    partial_value = jnp.dot(masked_bf, jac_block, preferred_element_type=jnp.float32)
    owned = lax.psum_scatter(
        partial_value.astype(jnp.bfloat16), "wave", scatter_dimension=1, tiled=True
    ).astype(jnp.float32)
    return lax.all_gather(owned, "wave", axis=1, tiled=True)


def reduce_scalars(values):
    return lax.psum(values, "section")


def shards(nominal_field, sensitivity, aberrations, jacobian, tile_mask, regul, initial_commands):
    components = jacobian.shape[1]
    pixels = jacobian.shape[2]
    block_width = jacobian.shape[3]
    row_count = components * pixels
    share_rows = row_count // lax.axis_size("section")
    row_start = lax.axis_index("section") * share_rows
    jac_block = jacobian.reshape(row_count, block_width)
    tile_count = tile_mask.shape[1]
    weight_full = jnp.broadcast_to(
        tile_mask[0].astype(jnp.float32)[None, :, None],
        (components, tile_count, pixels // tile_count),
    ).reshape(1, row_count)
    weight = lax.dynamic_slice_in_dim(weight_full, row_start, share_rows, 1)
    mode_count = sensitivity.shape[1]
    sens_share = lax.dynamic_slice_in_dim(
        sensitivity.reshape(mode_count, row_count), row_start, share_rows, 1
    )
    nominal_share = lax.dynamic_slice_in_dim(
        nominal_field.reshape(1, row_count), row_start, share_rows, 1
    )
    field_now = nominal_share + jnp.dot(aberrations, sens_share, preferred_element_type=jnp.float32)
    commands = initial_commands
    field_now = field_now + to_section_image(commands.astype(jnp.bfloat16), jac_block)
    for iteration in range(ITERS):
        residual = -back_of((weight * field_now).astype(jnp.bfloat16), jac_block)
        direction = residual
        change = jnp.zeros_like(residual)
        field_step = jnp.zeros_like(field_now)
        norm_now = reduce_scalars(jnp.sum(residual * residual, axis=1))
        for inner_step in range(CG):
            image_now = to_section_image(direction.astype(jnp.bfloat16), jac_block)
            applied = (
                back_of((weight * image_now).astype(jnp.bfloat16), jac_block)
                + regul[None, :] * direction
            )
            curvature = reduce_scalars(jnp.sum(direction * applied, axis=1))
            step_len = norm_now / (curvature + epsilon)
            residual = residual - step_len[:, None] * applied
            norm_next = reduce_scalars(jnp.sum(residual * residual, axis=1))
            change = change + step_len[:, None] * direction
            field_step = field_step + step_len[:, None] * image_now
            direction = residual + (norm_next / (norm_now + epsilon))[:, None] * direction
            norm_now = norm_next
        commands = commands + change
        field_now = field_now + field_step
    whole_field = lax.all_gather(
        field_now.astype(jnp.bfloat16), "section", axis=1, tiled=True
    ).astype(field_now.dtype)
    return (commands, whole_field.reshape(whole_field.shape[0], 1, components, pixels))


def solution(mesh):
    placed = (
        P("wave", None, None),
        P("wave", None, None, None),
        P("groups", None),
        P("wave", None, None, "section"),
        P("wave", None),
        P("section"),
        P("groups", "section"),
    )
    return jax.shard_map(
        shards,
        mesh=mesh,
        in_specs=placed,
        out_specs=(P("groups", "section"), P("groups", "wave", None, None)),
        check_vma=False,
    )
```

profile of v0, /device:TPU:0, one launch (start us, length us, event | category | flops | bytes accessed | tf_op | source)
XLA Modules:
  0.0 1012.5 jit_solution(16985530834480768755)
XLA Ops:
  14.9 22.3 %reduce-scatter.24.cloned.1.call-done = bf16[64,512]{1,0:T(8,128)(2,1)} async-done(((bf16[64,2048]{1,0:T(8,128)(2,1)}), bf16[64,512]{1,0:T(8,128)(2,1)}) %reduce-scatter.24.cloned.1.call-update) | async-done | bytes 65552 | tf_op jit(solution)/shard_map/reduce_scatter | solution.py:17
  49.7 19.8 %reduce-scatter.26.cloned.1.call-done = bf16[64,512]{1,0:T(8,128)(2,1)} async-done(((bf16[64,2048]{1,0:T(8,128)(2,1)}), bf16[64,512]{1,0:T(8,128)(2,1)}) %reduce-scatter.26.cloned.1.call-update) | async-done | bytes 65552 | tf_op jit(solution)/shard_map/reduce_scatter | solution.py:25
  92.2 18.9 %reduce-scatter.28.cloned.1.call-done = bf16[64,512]{1,0:T(8,128)(2,1)} async-done(((bf16[64,2048]{1,0:T(8,128)(2,1)}), bf16[64,512]{1,0:T(8,128)(2,1)}) %reduce-scatter.28.cloned.1.call-update) | async-done | bytes 65552 | tf_op jit(solution)/shard_map/reduce_scatter | solution.py:17
  123.5 19.8 %reduce-scatter.30.cloned.1.call-done = bf16[64,512]{1,0:T(8,128)(2,1)} async-done(((bf16[64,2048]{1,0:T(8,128)(2,1)}), bf16[64,512]{1,0:T(8,128)(2,1)}) %reduce-scatter.30.cloned.1.call-update) | async-done | bytes 65552 | tf_op jit(solution)/shard_map/reduce_scatter | solution.py:25
  178.9 18.1 %reduce-scatter.32.cloned.1.call-done = bf16[64,512]{1,0:T(8,128)(2,1)} async-done(((bf16[64,2048]{1,0:T(8,128)(2,1)}), bf16[64,512]{1,0:T(8,128)(2,1)}) %reduce-scatter.32.cloned.1.call-update) | async-done | bytes 65552 | tf_op jit(solution)/shard_map/reduce_scatter | solution.py:17
  209.9 19.8 %reduce-scatter.34.cloned.1.call-done = bf16[64,512]{1,0:T(8,128)(2,1)} async-done(((bf16[64,2048]{1,0:T(8,128)(2,1)}), bf16[64,512]{1,0:T(8,128)(2,1)}) %reduce-scatter.34.cloned.1.call-update) | async-done | bytes 65552 | tf_op jit(solution)/shard_map/reduce_scatter | solution.py:25
  266.0 18.2 %reduce-scatter.36.cloned.1.call-done = bf16[64,512]{1,0:T(8,128)(2,1)} async-done(((bf16[64,2048]{1,0:T(8,128)(2,1)}), bf16[64,512]{1,0:T(8,128)(2,1)}) %reduce-scatter.36.cloned.1.call-update) | async-done | bytes 65552 | tf_op jit(solution)/shard_map/reduce_scatter | solution.py:17
  296.6 19.8 %reduce-scatter.38.cloned.1.call-done = bf16[64,512]{1,0:T(8,128)(2,1)} async-done(((bf16[64,2048]{1,0:T(8,128)(2,1)}), bf16[64,512]{1,0:T(8,128)(2,1)}) %reduce-scatter.38.cloned.1.call-update) | async-done | bytes 65552 | tf_op jit(solution)/shard_map/reduce_scatter | solution.py:25
  317.2 15.3 %all_gather.82 = f32[64,2048]{1,0:T(8,128)S(1)} all-gather(f32[64,512]{1,0:T(8,128)S(1)} %convert_element_type.246), channel_id=1, replica_groups=mesh['groups'=2,'wave'=4,'section'=4] {'wave'}, dimensions={1}, use_global_device_ids=true | all-gather | bytes 655360 | tf_op jit(solution)/shard_map/all_gather | solution.py:28
  352.3 18.0 %reduce-scatter.40.cloned.1.call-done = bf16[64,512]{1,0:T(8,128)(2,1)} async-done(((bf16[64,2048]{1,0:T(8,128)(2,1)}), bf16[64,512]{1,0:T(8,128)(2,1)}) %reduce-scatter.40.cloned.1.call-update) | async-done | bytes 65552 | tf_op jit(solution)/shard_map/reduce_scatter | solution.py:17
  382.7 19.8 %reduce-scatter.42.cloned.1.call-done = bf16[64,512]{1,0:T(8,128)(2,1)} async-done(((bf16[64,2048]{1,0:T(8,128)(2,1)}), bf16[64,512]{1,0:T(8,128)(2,1)}) %reduce-scatter.42.cloned.1.call-update) | async-done | bytes 65552 | tf_op jit(solution)/shard_map/reduce_scatter | solution.py:25
  438.3 18.2 %reduce-scatter.44.cloned.1.call-done = bf16[64,512]{1,0:T(8,128)(2,1)} async-done(((bf16[64,2048]{1,0:T(8,128)(2,1)}), bf16[64,512]{1,0:T(8,128)(2,1)}) %reduce-scatter.44.cloned.1.call-update) | async-done | bytes 65552 | tf_op jit(solution)/shard_map/reduce_scatter | solution.py:17
  468.9 19.8 %reduce-scatter.46.cloned.1.call-done = bf16[64,512]{1,0:T(8,128)(2,1)} async-done(((bf16[64,2048]{1,0:T(8,128)(2,1)}), bf16[64,512]{1,0:T(8,128)(2,1)}) %reduce-scatter.46.cloned.1.call-update) | async-done | bytes 65552 | tf_op jit(solution)/shard_map/reduce_scatter | solution.py:25
  522.4 18.5 %reduce-scatter.48.cloned.1.call-done = bf16[64,512]{1,0:T(8,128)(2,1)} async-done(((bf16[64,2048]{1,0:T(8,128)(2,1)}), bf16[64,512]{1,0:T(8,128)(2,1)}) %reduce-scatter.48.cloned.1.call-update) | async-done | bytes 65552 | tf_op jit(solution)/shard_map/reduce_scatter | solution.py:25
  563.8 18.8 %reduce-scatter.50.cloned.1.call-done = bf16[64,512]{1,0:T(8,128)(2,1)} async-done(((bf16[64,2048]{1,0:T(8,128)(2,1)}), bf16[64,512]{1,0:T(8,128)(2,1)}) %reduce-scatter.50.cloned.1.call-update) | async-done | bytes 65552 | tf_op jit(solution)/shard_map/reduce_scatter | solution.py:17
  595.0 19.8 %reduce-scatter.52.cloned.1.call-done = bf16[64,512]{1,0:T(8,128)(2,1)} async-done(((bf16[64,2048]{1,0:T(8,128)(2,1)}), bf16[64,512]{1,0:T(8,128)(2,1)}) %reduce-scatter.52.cloned.1.call-update) | async-done | bytes 65552 | tf_op jit(solution)/shard_map/reduce_scatter | solution.py:25
  650.4 18.4 %reduce-scatter.54.cloned.1.call-done = bf16[64,512]{1,0:T(8,128)(2,1)} async-done(((bf16[64,2048]{1,0:T(8,128)(2,1)}), bf16[64,512]{1,0:T(8,128)(2,1)}) %reduce-scatter.54.cloned.1.call-update) | async-done | bytes 65552 | tf_op jit(solution)/shard_map/reduce_scatter | solution.py:17
  681.4 19.8 %reduce-scatter.56.cloned.1.call-done = bf16[64,512]{1,0:T(8,128)(2,1)} async-done(((bf16[64,2048]{1,0:T(8,128)(2,1)}), bf16[64,512]{1,0:T(8,128)(2,1)}) %reduce-scatter.56.cloned.1.call-update) | async-done | bytes 65552 | tf_op jit(solution)/shard_map/reduce_scatter | solution.py:25
  739.3 18.5 %reduce-scatter.58.cloned.1.call-done = bf16[64,512]{1,0:T(8,128)(2,1)} async-done(((bf16[64,2048]{1,0:T(8,128)(2,1)}), bf16[64,512]{1,0:T(8,128)(2,1)}) %reduce-scatter.58.cloned.1.call-update) | async-done | bytes 65552 | tf_op jit(solution)/shard_map/reduce_scatter | solution.py:17
  770.2 19.7 %reduce-scatter.60.cloned.1.call-done = bf16[64,512]{1,0:T(8,128)(2,1)} async-done(((bf16[64,2048]{1,0:T(8,128)(2,1)}), bf16[64,512]{1,0:T(8,128)(2,1)}) %reduce-scatter.60.cloned.1.call-update) | async-done | bytes 65552 | tf_op jit(solution)/shard_map/reduce_scatter | solution.py:25
  829.5 18.3 %reduce-scatter.62.cloned.1.call-done = bf16[64,512]{1,0:T(8,128)(2,1)} async-done(((bf16[64,2048]{1,0:T(8,128)(2,1)}), bf16[64,512]{1,0:T(8,128)(2,1)}) %reduce-scatter.62.cloned.1.call-update) | async-done | bytes 65552 | tf_op jit(solution)/shard_map/reduce_scatter | solution.py:17
  860.2 19.8 %reduce-scatter.64.cloned.1.call-done = bf16[64,512]{1,0:T(8,128)(2,1)} async-done(((bf16[64,2048]{1,0:T(8,128)(2,1)}), bf16[64,512]{1,0:T(8,128)(2,1)}) %reduce-scatter.64.cloned.1.call-update) | async-done | bytes 65552 | tf_op jit(solution)/shard_map/reduce_scatter | solution.py:25
  918.8 18.3 %reduce-scatter.66.cloned.1.call-done = bf16[64,512]{1,0:T(8,128)(2,1)} async-done(((bf16[64,2048]{1,0:T(8,128)(2,1)}), bf16[64,512]{1,0:T(8,128)(2,1)}) %reduce-scatter.66.cloned.1.call-update) | async-done | bytes 65552 | tf_op jit(solution)/shard_map/reduce_scatter | solution.py:17
  949.4 19.8 %reduce-scatter.68.cloned.1.call-done = bf16[64,512]{1,0:T(8,128)(2,1)} async-done(((bf16[64,2048]{1,0:T(8,128)(2,1)}), bf16[64,512]{1,0:T(8,128)(2,1)}) %reduce-scatter.68.cloned.1.call-update) | async-done | bytes 65552 | tf_op jit(solution)/shard_map/reduce_scatter | solution.py:25
  (235 shorter events, 540.2 us)
Async XLA Ops:
  7.2 30.0 %reduce-scatter.24.cloned.1.call-start = ((), (), s32[]{:S(2)}) async-start(), calls=%async_computation.23 | async-start | bytes 327680 | tf_op jit(solution)/shard_map/reduce_scatter | solution.py:17
  14.3 55.3 %reduce-scatter.26.cloned.1.call-start = ((), (), s32[]{:S(2)}) async-start(), calls=%async_computation.24 | async-start | bytes 327680 | tf_op jit(solution)/shard_map/reduce_scatter | solution.py:25
  49.7 61.4 %reduce-scatter.28.cloned.1.call-start = ((), (), s32[]{:S(2)}) async-start(), calls=%async_computation.25 | async-start | bytes 327680 | tf_op jit(solution)/shard_map/reduce_scatter | solution.py:17
  92.1 51.1 %reduce-scatter.30.cloned.1.call-start = ((), (), s32[]{:S(2)}) async-start(), calls=%async_computation.26 | async-start | bytes 327680 | tf_op jit(solution)/shard_map/reduce_scatter | solution.py:25
  123.4 73.6 %reduce-scatter.32.cloned.1.call-start = ((), (), s32[]{:S(2)}) async-start(), calls=%async_computation.27 | async-start | bytes 327680 | tf_op jit(solution)/shard_map/reduce_scatter | solution.py:17
  178.9 50.8 %reduce-scatter.34.cloned.1.call-start = ((), (), s32[]{:S(2)}) async-start(), calls=%async_computation.28 | async-start | bytes 327680 | tf_op jit(solution)/shard_map/reduce_scatter | solution.py:25
  209.9 74.4 %reduce-scatter.36.cloned.1.call-start = ((), (), s32[]{:S(2)}) async-start(), calls=%async_computation.29 | async-start | bytes 327680 | tf_op jit(solution)/shard_map/reduce_scatter | solution.py:17
  251.8 258.7 %copy-start.18 = (f32[64]{0:T(128)}, f32[64]{0:T(128)S(1)}, u32[]{:S(2)}) copy-start(f32[64]{0:T(128)S(1)} %add_divide_fusion.15) | copy-start | bytes 772
  266.0 50.4 %reduce-scatter.38.cloned.1.call-start = ((), (), s32[]{:S(2)}) async-start(), calls=%async_computation.30 | async-start | bytes 327680 | tf_op jit(solution)/shard_map/reduce_scatter | solution.py:25
  296.5 73.7 %reduce-scatter.40.cloned.1.call-start = ((), (), s32[]{:S(2)}) async-start(), calls=%async_computation.31 | async-start | bytes 327680 | tf_op jit(solution)/shard_map/reduce_scatter | solution.py:17
  352.2 50.2 %reduce-scatter.42.cloned.1.call-start = ((), (), s32[]{:S(2)}) async-start(), calls=%async_computation.32 | async-start | bytes 327680 | tf_op jit(solution)/shard_map/reduce_scatter | solution.py:25
  382.6 73.9 %reduce-scatter.44.cloned.1.call-start = ((), (), s32[]{:S(2)}) async-start(), calls=%async_computation.33 | async-start | bytes 327680 | tf_op jit(solution)/shard_map/reduce_scatter | solution.py:17
  438.2 50.5 %reduce-scatter.46.cloned.1.call-start = ((), (), s32[]{:S(2)}) async-start(), calls=%async_computation.34 | async-start | bytes 327680 | tf_op jit(solution)/shard_map/reduce_scatter | solution.py:25
  468.9 72.1 %reduce-scatter.48.cloned.1.call-start = ((), (), s32[]{:S(2)}) async-start(), calls=%async_computation.35 | async-start | bytes 327680 | tf_op jit(solution)/shard_map/reduce_scatter | solution.py:25
  522.4 60.2 %reduce-scatter.50.cloned.1.call-start = ((), (), s32[]{:S(2)}) async-start(), calls=%async_computation.36 | async-start | bytes 327680 | tf_op jit(solution)/shard_map/reduce_scatter | solution.py:17
  563.8 51.0 %reduce-scatter.52.cloned.1.call-start = ((), (), s32[]{:S(2)}) async-start(), calls=%async_computation.37 | async-start | bytes 327680 | tf_op jit(solution)/shard_map/reduce_scatter | solution.py:25
  594.9 73.9 %reduce-scatter.54.cloned.1.call-start = ((), (), s32[]{:S(2)}) async-start(), calls=%async_computation.38 | async-start | bytes 327680 | tf_op jit(solution)/shard_map/reduce_scatter | solution.py:17
  650.3 50.8 %reduce-scatter.56.cloned.1.call-start = ((), (), s32[]{:S(2)}) async-start(), calls=%async_computation.39 | async-start | bytes 327680 | tf_op jit(solution)/shard_map/reduce_scatter | solution.py:25
  681.3 76.5 %reduce-scatter.58.cloned.1.call-start = ((), (), s32[]{:S(2)}) async-start(), calls=%async_computation.40 | async-start | bytes 327680 | tf_op jit(solution)/shard_map/reduce_scatter | solution.py:17
  739.3 50.6 %reduce-scatter.60.cloned.1.call-start = ((), (), s32[]{:S(2)}) async-start(), calls=%async_computation.41 | async-start | bytes 327680 | tf_op jit(solution)/shard_map/reduce_scatter | solution.py:25
  770.1 77.7 %reduce-scatter.62.cloned.1.call-start = ((), (), s32[]{:S(2)}) async-start(), calls=%async_computation.42 | async-start | bytes 327680 | tf_op jit(solution)/shard_map/reduce_scatter | solution.py:17
  829.5 50.5 %reduce-scatter.64.cloned.1.call-start = ((), (), s32[]{:S(2)}) async-start(), calls=%async_computation.43 | async-start | bytes 327680 | tf_op jit(solution)/shard_map/reduce_scatter | solution.py:25
  860.2 76.9 %reduce-scatter.66.cloned.1.call-start = ((), (), s32[]{:S(2)}) async-start(), calls=%async_computation.44 | async-start | bytes 327680 | tf_op jit(solution)/shard_map/reduce_scatter | solution.py:17
  918.7 50.5 %reduce-scatter.68.cloned.1.call-start = ((), (), s32[]{:S(2)}) async-start(), calls=%async_computation.45 | async-start | bytes 327680 | tf_op jit(solution)/shard_map/reduce_scatter | solution.py:25
  (25 other events, 1106.1 us)
Sparse Core Ops, SparseCore 0:
  14.4 22.7 reduce-scatter.23
  49.8 19.7 reduce-scatter.25
  92.2 18.7 reduce-scatter.27
  123.5 19.6 reduce-scatter.29
  179.0 18.0 reduce-scatter.31
  210.0 19.6 reduce-scatter.33
  266.1 18.0 reduce-scatter.35
  296.7 19.6 reduce-scatter.37
  352.4 17.8 reduce-scatter.39
  382.7 19.6 reduce-scatter.41
  438.3 18.0 reduce-scatter.43
  469.0 19.6 reduce-scatter.45
  522.5 18.4 reduce-scatter.47
  563.9 18.6 reduce-scatter.49
  595.0 19.6 reduce-scatter.51
  650.4 18.3 reduce-scatter.53
  681.4 19.6 reduce-scatter.55
  739.4 18.3 reduce-scatter.57
  770.2 19.5 reduce-scatter.59
  829.6 18.1 reduce-scatter.61
  860.3 19.6 reduce-scatter.63
  918.9 18.1 reduce-scatter.65
  949.5 19.6 reduce-scatter.67
where the time goes:
time: 1020 us; the launch traced here: 1010 us
  waiting for transfers between devices  442 us (43%)
  blocking collectives  369 us (36%)
  matrix products  144 us (14%)
  other arithmetic  38.1 us (4%)
  between operations  14.9 us (1%)
    reduce_scatter x12, waiting for transfers between devices, back_of(): lax.psum_scatter(partial_value.astype(jnp.bfloat16), 'wave', scatter_dime...  236 us
    reduce_scatter x11, waiting for transfers between devices, to_section_image(): lax.psum_scatter(partial_value.astype(jnp.bfloat16), 'section', scatter_d...  206 us
    all_gather x12, blocking collectives, back_of(): return lax.all_gather(owned, 'wave', axis=1, tiled=True)  181 us
    psum x18, blocking collectives, reduce_scalars(): return lax.psum(values, 'section')  111 us
    dot_general x11, matrix products, to_section_image(): lax.dot_general(command_bf, jac_block, (((1,), (1,)), ((), ())), preferre...  75.1 us
    all_gather x12, blocking collectives, back_of(): masked_bf = lax.all_gather(masked_share, 'section', axis=1, tiled=True)  70.3 us
    dot_general x12, matrix products, back_of(): jnp.dot(masked_bf, jac_block, preferred_element_type=jnp.float32)  67.9 us
  transfers between devices with their start and end apart: 23, of which 23 were waited for; matrix products, arithmetic and copies ran while one was open for 0% of the time, Pallas kernels for 0%

commit v1 on v0

--- a/solution.py
+++ b/solution.py
@@ -1,11 +1,16 @@
+import functools
+
 import jax
 import jax.numpy as jnp
 from jax import lax
+from jax.experimental import pallas as pl
+from jax.experimental.pallas import tpu as pltpu
 from jax.sharding import PartitionSpec as P
 
 ITERS = 2
 CG = 5
-
+LANES = 128
+CHUNKS = 2
 
 epsilon = 1e-06
 
@@ -32,7 +37,7 @@
     return lax.psum(values, "section")
 
 
-def shards(nominal_field, sensitivity, aberrations, jacobian, tile_mask, regul, initial_commands):
+def general_shards(nominal_field, sensitivity, aberrations, jacobian, tile_mask, regul, initial_commands):
     components = jacobian.shape[1]
     pixels = jacobian.shape[2]
     block_width = jacobian.shape[3]
@@ -84,6 +89,344 @@
     return (commands, whole_field.reshape(whole_field.shape[0], 1, components, pixels))
 
 
+def control_kernel(
+    n,
+    rb,
+    jac_hbm,
+    base_ref,
+    start_ref,
+    regul_ref,
+    weight_ref,
+    cmd_ref,
+    out_ref,
+    jac,
+    probe,
+    masked,
+    sec_part,
+    sec_recv,
+    wav_part,
+    wav_recv,
+    image,
+    field,
+    residual,
+    direction,
+    acc,
+    dots_send,
+    dots_recv,
+    norm,
+    steps,
+    jac_sem,
+    sec_ss,
+    sec_rs,
+    msk_ss,
+    msk_rs,
+    wav_ss,
+    wav_rs,
+    prb_ss,
+    prb_rs,
+    dot_ss,
+    dot_rs,
+    stp_ss,
+    stp_rs,
+):
+    f32, bf16 = jnp.float32, jnp.bfloat16
+    rows, acts = jac.shape
+    reals = n * rb
+    rc, ac = rows // CHUNKS, acts // CHUNKS
+    sec, wav = lax.axis_index("section"), lax.axis_index("wave")
+    sec_peer = [lax.rem(sec + k, n) for k in range(1, n)]
+    wav_peer = [lax.rem(wav + k, n) for k in range(1, n)]
+
+    load = pltpu.make_async_copy(jac_hbm, jac, jac_sem)
+    load.start()
+    barrier = pltpu.get_barrier_semaphore()
+    for p in sec_peer:
+        pl.semaphore_signal(
+            barrier, inc=1, device_id={"section": p}, device_id_type=pl.DeviceIdType.MESH
+        )
+    for p in wav_peer:
+        pl.semaphore_signal(
+            barrier, inc=1, device_id={"wave": p}, device_id_type=pl.DeviceIdType.MESH
+        )
+    pl.semaphore_wait(barrier, 2 * (n - 1))
+
+    def to_section(k, src, dst, ss, rs):
+        return pltpu.make_async_remote_copy(
+            src_ref=src, dst_ref=dst, send_sem=ss, recv_sem=rs,
+            device_id={"section": sec_peer[k]}, device_id_type=pl.DeviceIdType.MESH,
+        )
+
+    def to_wave(k, src, dst, ss, rs):
+        return pltpu.make_async_remote_copy(
+            src_ref=src, dst_ref=dst, send_sem=ss, recv_sem=rs,
+            device_id={"wave": wav_peer[k]}, device_id_type=pl.DeviceIdType.MESH,
+        )
+
+    peers = range(n - 1)
+
+    def sec_copy(j, k):
+        return to_section(k, sec_part.at[j, sec_peer[k]], sec_recv.at[j, k], sec_ss.at[j, k], sec_rs.at[j, k])
+
+    def msk_copy(j, k):
+        return to_section(k, masked.at[j, sec], masked.at[j, sec], msk_ss.at[j, k], msk_rs.at[j, k])
+
+    def wav_copy(c, k):
+        return to_wave(k, wav_part.at[c, wav_peer[k]], wav_recv.at[c, k], wav_ss.at[c, k], wav_rs.at[c, k])
+
+    def prb_copy(slot, c, k):
+        return to_wave(
+            k, probe.at[slot, c, wav], probe.at[slot, c, wav], prb_ss.at[c, k], prb_rs.at[c, k]
+        )
+
+    def dot_copy(k):
+        return to_section(k, dots_send, dots_recv.at[k], dot_ss.at[k], dot_rs.at[k])
+
+    def stp_copy(k):
+        return to_wave(k, steps.at[wav], steps.at[wav], stp_ss.at[k], stp_rs.at[k])
+
+    def make_image(slot, arrive):
+        for c in range(CHUNKS):
+            arrive(c)
+            lhs = probe[slot, c].reshape(reals, ac)
+            for j in range(CHUNKS):
+                part = lax.dot_general(
+                    lhs,
+                    jac[j * rc:(j + 1) * rc, c * ac:(c + 1) * ac],
+                    (((1,), (1,)), ((), ())),
+                    preferred_element_type=f32,
+                )
+                if c:
+                    part = acc[:, j * rc:(j + 1) * rc] + part
+                if c < CHUNKS - 1:
+                    acc[:, j * rc:(j + 1) * rc] = part
+                else:
+                    sec_part[j] = part.astype(bf16).reshape(n, rb, rc)
+                    for k in peers:
+                        sec_copy(j, k).start()
+
+    def take_image(j):
+        for k in peers:
+            sec_copy(j, k).wait()
+        total = sec_part[j, sec].astype(f32)
+        for k in peers:
+            total = total + sec_recv[j, k].astype(f32)
+        return total
+
+    def send_masked(j, values):
+        masked[j, sec] = (weight_ref[:, j * rc:(j + 1) * rc] * values).astype(bf16)
+        for k in peers:
+            msk_copy(j, k).start()
+
+    def make_back():
+        for j in range(CHUNKS):
+            for k in peers:
+                msk_copy(j, k).wait()
+            lhs = masked[j].reshape(reals, rc)
+            for c in range(CHUNKS):
+                part = jnp.dot(
+                    lhs,
+                    jac[j * rc:(j + 1) * rc, c * ac:(c + 1) * ac],
+                    preferred_element_type=f32,
+                )
+                if j:
+                    part = acc[:, c * ac:(c + 1) * ac] + part
+                if j < CHUNKS - 1:
+                    acc[:, c * ac:(c + 1) * ac] = part
+                else:
+                    wav_part[c] = part.astype(bf16).reshape(n, rb, ac)
+                    for k in peers:
+                        wav_copy(c, k).start()
+
+    def take_back(c):
+        for k in peers:
+            wav_copy(c, k).wait()
+        total = wav_part[c, wav].astype(f32)
+        for k in peers:
+            total = total + wav_recv[c, k].astype(f32)
+        return total
+
+    lane = lax.broadcasted_iota(jnp.int32, (rb, LANES), 1)
+
+    def reduce_dots(values):
+        packed = jnp.zeros((rb, LANES), f32)
+        for at, value in enumerate(values):
+            packed = jnp.where(lane == at, value, packed)
+        dots_send[...] = packed
+        for k in peers:
+            dot_copy(k).start()
+        for k in peers:
+            dot_copy(k).wait()
+        total = dots_send[...]
+        for k in peers:
+            total = total + dots_recv[k]
+        return [total[:, at:at + 1] for at in range(len(values))]
+
+    def row_sum(values):
+        return jnp.sum(values, axis=1, keepdims=True)
+
+    def send_probe(slot, c, values):
+        probe[slot, c, wav] = values.astype(bf16)
+        for k in peers:
+            prb_copy(slot, c, k).start()
+
+    def take_steps(slot):
+        for k in peers:
+            stp_copy(k).wait()
+        for j in range(CHUNKS):
+            field[j] = field[j] + steps[sec][:, 0:1] * image[j]
+        column = steps[...].reshape(reals, LANES)[:, 0:1]
+        for c in range(CHUNKS):
+            cols = slice(c * ac, (c + 1) * ac)
+            cmd_ref[:, cols] = cmd_ref[:, cols] + column * probe[slot, c].reshape(reals, ac).astype(f32)
+
+    cmd_ref[...] = start_ref[...]
+    for c in range(CHUNKS):
+        probe[0, c] = start_ref[:, c * ac:(c + 1) * ac].astype(bf16).reshape(n, rb, ac)
+    load.wait()
+    make_image(0, lambda c: None)
+    for j in range(CHUNKS):
+        field[j] = base_ref[:, j * rc:(j + 1) * rc] + take_image(j)
+
+    def iteration(_, carry):
+        for j in range(CHUNKS):
+            send_masked(j, field[j])
+        make_back()
+        square = jnp.zeros((rb, 1), f32)
+        for c in range(CHUNKS):
+            start = -take_back(c)
+            residual[c] = start
+            direction[c] = start
+            send_probe(0, c, start)
+            square = square + row_sum(start * start)
+        (first,) = reduce_dots([square])
+        norm[...] = jnp.broadcast_to(first, (rb, LANES))
+
+        def cg_step(step, carry):
+            slot = lax.rem(step, 2)
+
+            def arrive(c):
+                for k in peers:
+                    prb_copy(slot, c, k).wait()
+
+            make_image(slot, arrive)
+
+            @pl.when(step > 0)
+            def _():
+                take_steps(1 - slot)
+
+            for j in range(CHUNKS):
+                total = take_image(j)
+                image[j] = total
+                send_masked(j, total)
+            make_back()
+            dd = jnp.zeros((rb, 1), f32)
+            ra, aa = dd, dd
+            for c in range(CHUNKS):
+                along = direction[c]
+                applied = take_back(c) + regul_ref[:, c * ac:(c + 1) * ac] * along
+                acc[0:rb, c * ac:(c + 1) * ac] = applied
+                dd = dd + row_sum(along * applied)
+                ra = ra + row_sum(residual[c] * applied)
+                aa = aa + row_sum(applied * applied)
+            curvature, ra, aa = reduce_dots([dd, ra, aa])
+            norm_now = norm[:, 0:1]
+            step_len = norm_now / (curvature + epsilon)
+            norm_next = jnp.maximum(norm_now + step_len * (step_len * aa - 2.0 * ra), 0.0)
+            ratio = norm_next / (norm_now + epsilon)
+            norm[...] = jnp.broadcast_to(norm_next, (rb, LANES))
+            steps[wav] = jnp.broadcast_to(step_len, (rb, LANES))
+            for k in peers:
+                stp_copy(k).start()
+
+            @pl.when(step < CG - 1)
+            def _():
+                for c in range(CHUNKS):
+                    after = residual[c] - step_len * acc[0:rb, c * ac:(c + 1) * ac]
+                    residual[c] = after
+                    ahead = after + ratio * direction[c]
+                    direction[c] = ahead
+                    send_probe(1 - slot, c, ahead)
+
+            return carry
+
+        lax.fori_loop(0, CG, cg_step, 0)
+        take_steps((CG - 1) % 2)
+        return carry
+
+    lax.fori_loop(0, ITERS, iteration, 0)
+
+    for j in range(CHUNKS):
+        masked[j, sec] = field[j].astype(bf16)
+        for k in peers:
+            msk_copy(j, k).start()
+    for j in range(CHUNKS):
+        for k in peers:
+            msk_copy(j, k).wait()
+        out_ref[:, j * rc:(j + 1) * rc] = masked[j].reshape(reals, rc).astype(f32)
+
+
+def kernel_shards(nominal_field, sensitivity, aberrations, jacobian, tile_mask, regul, initial_commands):
+    f32, bf16 = jnp.float32, jnp.bfloat16
+    components, pixels, acts = jacobian.shape[1:]
+    rows = components * pixels
+    reals = initial_commands.shape[0]
+    n = lax.axis_size("section")
+    rb = reals // n
+    rc, ac = rows // CHUNKS, acts // CHUNKS
+    tile_count = tile_mask.shape[1]
+    weight = jnp.broadcast_to(
+        tile_mask[0].astype(f32)[None, :, None],
+        (components, tile_count, pixels // tile_count),
+    ).reshape(1, rows)
+    own = lax.dynamic_slice_in_dim(aberrations, lax.axis_index("section") * rb, rb, 0)
+    base = nominal_field[0][None] + lax.dot_general(
+        own, sensitivity[0], (((1,), (0,)), ((), ())), preferred_element_type=f32
+    )
+    vmem = pl.BlockSpec(memory_space=pltpu.VMEM)
+    dma = pltpu.SemaphoreType.DMA
+    commands, field = pl.pallas_call(
+        functools.partial(control_kernel, n, rb),
+        out_shape=(
+            jax.ShapeDtypeStruct((reals, acts), f32),
+            jax.ShapeDtypeStruct((reals, rows), f32),
+        ),
+        in_specs=[pl.BlockSpec(memory_space=pl.ANY), vmem, vmem, vmem, vmem],
+        out_specs=(vmem, vmem),
+        scratch_shapes=[
+            pltpu.VMEM((rows, acts), bf16),
+            pltpu.VMEM((2, CHUNKS, n, rb, ac), bf16),
+            pltpu.VMEM((CHUNKS, n, rb, rc), bf16),
+            pltpu.VMEM((CHUNKS, n, rb, rc), bf16),
+            pltpu.VMEM((CHUNKS, n - 1, rb, rc), bf16),
+            pltpu.VMEM((CHUNKS, n, rb, ac), bf16),
+            pltpu.VMEM((CHUNKS, n - 1, rb, ac), bf16),
+            pltpu.VMEM((CHUNKS, rb, rc), f32),
+            pltpu.VMEM((CHUNKS, rb, rc), f32),
+            pltpu.VMEM((CHUNKS, rb, ac), f32),
+            pltpu.VMEM((CHUNKS, rb, ac), f32),
+            pltpu.VMEM((reals, max(rows, acts)), f32),
+            pltpu.VMEM((rb, LANES), f32),
+            pltpu.VMEM((n - 1, rb, LANES), f32),
+            pltpu.VMEM((rb, LANES), f32),
+            pltpu.VMEM((n, rb, LANES), f32),
+            dma(()),
+        ]
+        + [dma((CHUNKS, n - 1))] * 8
+        + [dma((n - 1,))] * 4,
+        compiler_params=pltpu.CompilerParams(
+            collective_id=0, has_side_effects=True, vmem_limit_bytes=40 * 1024 * 1024
+        ),
+        name="control_loop",
+    )(
+        jacobian.reshape(rows, acts),
+        base.reshape(rb, rows),
+        initial_commands,
+        regul[None, :],
+        weight,
+    )
+    return commands, field.reshape(reals, 1, components, pixels)
+
+
 def solution(mesh):
     placed = (
         P("wave", None, None),
@@ -94,8 +437,25 @@
         P("section"),
         P("groups", "section"),
     )
+
+    def choose(*args):
+        n, waves = mesh.shape["section"], mesh.shape["wave"]
+        reals = args[6].shape[0]
+        acts = args[3].shape[3]
+        rows = args[3].shape[1] * args[3].shape[2]
+        fits = (
+            n == waves
+            and n > 1
+            and reals % (16 * n) == 0
+            and acts % (LANES * CHUNKS) == 0
+            and rows % (LANES * CHUNKS) == 0
+            and rows * acts <= 2048 * 2048
+            and reals <= 64
+        )
+        return (kernel_shards if fits else general_shards)(*args)
+
     return jax.shard_map(
-        shards,
+        choose,
         mesh=mesh,
         in_specs=placed,
         out_specs=(P("groups", "section"), P("groups", "wave", None, None)),

time: 1020 us -> 327 us (0.32)
  waiting for transfers between devices: 442 us -> 0 us
  blocking collectives: 369 us -> 0 us
  Pallas kernels: 0 us -> 317 us
  matrix products: 144 us -> 1.24 us
  other arithmetic: 38.1 us -> 0.66 us
  between operations: 14.9 us -> 0.7 us
    reduce_scatter x23 -> x0, waiting for transfers between devices: 442 us -> none  [the longest x12 236 us: back_of(): lax.psum_scatter(partial_value.astype(jnp.bfloat16), 'wave', scatter_dime...]
    pallas_call x0 -> x1, Pallas kernels: none -> 317 us  [kernel_shards(): pl.pallas_call(functools.partial(control_kernel, n, rb), out_shape=(jax.S...]
    all_gather x25 -> x0, blocking collectives: 257 us -> none  [the longest x12 181 us: back_of(): return lax.all_gather(owned, 'wave', axis=1, tiled=True)]
    dot_general x24 -> x1, matrix products: 144 us -> 1.24 us  [kernel_shards(): lax.dot_general(own, sensitivity[0], (((1,), (0,)), ((), ())), preferred_...]
    psum x18 -> x0, blocking collectives: 111 us -> none  [reduce_scalars(): return lax.psum(values, 'section')]
    convert_element_type x25 -> x1, other arithmetic: 19.9 us -> 0.66 us  [kernel_shards(): tile_mask[0].astype(f32)[None, :, None]]
    reduce_sum x18 -> x0, other arithmetic: 11.1 us -> none  [the longest x8 7.2 us: shards(): norm_next = reduce_scalars(jnp.sum(residual * residual, axis=1))]
  transfers between devices with their start and end apart: 23 -> 0, of which waited for: 23 -> 0; matrix products, arithmetic and copies ran while one was open for 0% -> 0% of each run, Pallas kernels for 0% -> 0%
where the time goes in v1:
time: 327 us
  Pallas kernels  317 us (97%)
  local copies, waits for them, and re-layouts  6.84 us (2%)
    pallas_call x1, Pallas kernels, kernel_shards(): pl.pallas_call(functools.partial(control_kernel, n, rb), out_shape=(jax.S...  317 us

profile of v1, /device:TPU:0, one launch (start us, length us, event | category | flops | bytes accessed | tf_op | source)
XLA Modules:
  0.0 326.6 jit_solution(9962336930007418788)
XLA Ops:
  0.6 0.0 copy-start
  0.6 0.0 copy-start.2
  0.7 0.0 copy-start.3
  0.7 1.3 copy-done
  2.0 0.7 convert_bitcast_fusion
  2.7 0.1 broadcast_in_dim.10
  2.7 1.2 fusion.5
  4.0 0.0 copy-done.2
  4.0 0.0 copy-done.3
  4.0 0.0 copy-start.1
  4.0 3.4 %copy-done.1 = bf16[1,2,1024,2048]{3,2,1,0:T(8,128)(2,1)S(1)} copy-done((bf16[1,2,1024,2048]{3,2,1,0:T(8,128)(2,1)S(1)}, bf16[1,2,1024,2048]{3,2,1,0:T(8,128)(2,1)}, u32[]{:S(2)}) %copy-start.1) | copy-done | bytes 8388632
  7.4 317.2 %control_loop.1 = (f32[64,2048]{1,0:T(8,128)S(1)}, f32[64,2048]{1,0:T(8,128)S(1)}) custom-call(bf16[2048,2048]{1,0:T(8,128)(2,1)S(1)} %bitcast.15, f32[16,2048]{1,0:T(8,128)S(1)} %bitcast.16, f32[64,2048]{1,0:T(8,128)S(1)} %copy-done.2, f32[1,2048]{1,0:T(1,128)S(1)} %bitcast.18, f32[1,2048]{1,0:T(1,128)S(1)} %bitcast.17), custom_call_target="tpu_custom_call" | custom-call | tf_op jit(solution)/shard_map/control_loop/pallas_call | solution.py:387
  324.6 1.2 reshape.25
  325.8 0.8 copy.20
  (1 shorter events, 0.0 us)
Async XLA Ops:
  0.6 1.4 copy-start
  0.6 3.3 %copy-start.2 = (f32[64,2048]{1,0:T(8,128)S(1)}, f32[64,2048]{1,0:T(8,128)}, u32[]{:S(2)}) copy-start(f32[64,2048]{1,0:T(8,128)} %start_ref.1) | copy-start | bytes 1572868
  0.7 3.3 %copy-start.3 = (f32[2048]{0:T(1024)S(1)}, f32[2048]{0:T(1024)}, u32[]{:S(2)}) copy-start(f32[2048]{0:T(1024)} %param.12) | copy-start | bytes 24580
  4.0 3.4 %copy-start.1 = (bf16[1,2,1024,2048]{3,2,1,0:T(8,128)(2,1)S(1)}, bf16[1,2,1024,2048]{3,2,1,0:T(8,128)(2,1)}, u32[]{:S(2)}) copy-start(bf16[1,2,1024,2048]{3,2,1,0:T(8,128)(2,1)} %param.10) | copy-start | bytes 25165828

commit v2 on v1

v2 whole, which is shorter than its diff:
```python
import functools

import jax
import jax.numpy as jnp
from jax import lax
from jax.experimental import pallas as pl
from jax.experimental.pallas import tpu as pltpu
from jax.sharding import PartitionSpec as P

ITERS = 2
CG = 5
LANES = 128
CHUNKS = 2
STREAMS = 2

epsilon = 1e-06


def to_section_image(command_bf, jac_block):
    partial_value = lax.dot_general(
        command_bf, jac_block, (((1,), (1,)), ((), ())), preferred_element_type=jnp.float32
    )
    return lax.psum_scatter(
        partial_value.astype(jnp.bfloat16), "section", scatter_dimension=1, tiled=True
    ).astype(jnp.float32)


def back_of(masked_share, jac_block):
    masked_bf = lax.all_gather(masked_share, "section", axis=1, tiled=True)
    partial_value = jnp.dot(masked_bf, jac_block, preferred_element_type=jnp.float32)
    owned = lax.psum_scatter(
        partial_value.astype(jnp.bfloat16), "wave", scatter_dimension=1, tiled=True
    ).astype(jnp.float32)
    return lax.all_gather(owned, "wave", axis=1, tiled=True)


def reduce_scalars(values):
    return lax.psum(values, "section")


def general_shards(nominal_field, sensitivity, aberrations, jacobian, tile_mask, regul, initial_commands):
    components = jacobian.shape[1]
    pixels = jacobian.shape[2]
    block_width = jacobian.shape[3]
    row_count = components * pixels
    share_rows = row_count // lax.axis_size("section")
    row_start = lax.axis_index("section") * share_rows
    jac_block = jacobian.reshape(row_count, block_width)
    tile_count = tile_mask.shape[1]
    weight_full = jnp.broadcast_to(
        tile_mask[0].astype(jnp.float32)[None, :, None],
        (components, tile_count, pixels // tile_count),
    ).reshape(1, row_count)
    weight = lax.dynamic_slice_in_dim(weight_full, row_start, share_rows, 1)
    mode_count = sensitivity.shape[1]
    sens_share = lax.dynamic_slice_in_dim(
        sensitivity.reshape(mode_count, row_count), row_start, share_rows, 1
    )
    nominal_share = lax.dynamic_slice_in_dim(
        nominal_field.reshape(1, row_count), row_start, share_rows, 1
    )
    field_now = nominal_share + jnp.dot(aberrations, sens_share, preferred_element_type=jnp.float32)
    commands = initial_commands
    field_now = field_now + to_section_image(commands.astype(jnp.bfloat16), jac_block)
    for iteration in range(ITERS):
        residual = -back_of((weight * field_now).astype(jnp.bfloat16), jac_block)
        direction = residual
        change = jnp.zeros_like(residual)
        field_step = jnp.zeros_like(field_now)
        norm_now = reduce_scalars(jnp.sum(residual * residual, axis=1))
        for inner_step in range(CG):
            image_now = to_section_image(direction.astype(jnp.bfloat16), jac_block)
            applied = (
                back_of((weight * image_now).astype(jnp.bfloat16), jac_block)
                + regul[None, :] * direction
            )
            curvature = reduce_scalars(jnp.sum(direction * applied, axis=1))
            step_len = norm_now / (curvature + epsilon)
            residual = residual - step_len[:, None] * applied
            norm_next = reduce_scalars(jnp.sum(residual * residual, axis=1))
            change = change + step_len[:, None] * direction
            field_step = field_step + step_len[:, None] * image_now
            direction = residual + (norm_next / (norm_now + epsilon))[:, None] * direction
            norm_now = norm_next
        commands = commands + change
        field_now = field_now + field_step
    whole_field = lax.all_gather(
        field_now.astype(jnp.bfloat16), "section", axis=1, tiled=True
    ).astype(field_now.dtype)
    return (commands, whole_field.reshape(whole_field.shape[0], 1, components, pixels))


def control_kernel(
    n,
    rb,
    jac_hbm,
    base_ref,
    start_ref,
    regul_ref,
    weight_ref,
    cmd_ref,
    out_ref,
    jac,
    probe,
    masked,
    sec_part,
    sec_recv,
    wav_part,
    wav_recv,
    image,
    field,
    residual,
    direction,
    acc,
    applied_ref,
    dots_send,
    dots_recv,
    norm,
    steps,
    jac_sem,
    sec_ss,
    sec_rs,
    msk_ss,
    msk_rs,
    wav_ss,
    wav_rs,
    prb_ss,
    prb_rs,
    dot_ss,
    dot_rs,
    stp_ss,
    stp_rs,
):
    f32, bf16 = jnp.float32, jnp.bfloat16
    rows, acts = jac.shape
    reals = n * rb
    streams = range(STREAMS)
    rc, ac = rows // CHUNKS, acts // CHUNKS
    sec, wav = lax.axis_index("section"), lax.axis_index("wave")
    sec_peer = [lax.rem(sec + k, n) for k in range(1, n)]
    wav_peer = [lax.rem(wav + k, n) for k in range(1, n)]

    load = pltpu.make_async_copy(jac_hbm, jac, jac_sem)
    load.start()
    barrier = pltpu.get_barrier_semaphore()
    for p in sec_peer:
        pl.semaphore_signal(
            barrier, inc=1, device_id={"section": p}, device_id_type=pl.DeviceIdType.MESH
        )
    for p in wav_peer:
        pl.semaphore_signal(
            barrier, inc=1, device_id={"wave": p}, device_id_type=pl.DeviceIdType.MESH
        )
    pl.semaphore_wait(barrier, 2 * (n - 1))

    def to_section(k, src, dst, ss, rs):
        return pltpu.make_async_remote_copy(
            src_ref=src, dst_ref=dst, send_sem=ss, recv_sem=rs,
            device_id={"section": sec_peer[k]}, device_id_type=pl.DeviceIdType.MESH,
        )

    def to_wave(k, src, dst, ss, rs):
        return pltpu.make_async_remote_copy(
            src_ref=src, dst_ref=dst, send_sem=ss, recv_sem=rs,
            device_id={"wave": wav_peer[k]}, device_id_type=pl.DeviceIdType.MESH,
        )

    peers = range(n - 1)

    def sec_copy(h, j, k):
        return to_section(
            k, sec_part.at[h, j, sec_peer[k]], sec_recv.at[h, j, k], sec_ss.at[h, j, k], sec_rs.at[h, j, k]
        )

    def msk_copy(h, j, k):
        return to_section(
            k, masked.at[h, j, sec], masked.at[h, j, sec], msk_ss.at[h, j, k], msk_rs.at[h, j, k]
        )

    def wav_copy(h, c, k):
        return to_wave(
            k, wav_part.at[h, c, wav_peer[k]], wav_recv.at[h, c, k], wav_ss.at[h, c, k], wav_rs.at[h, c, k]
        )

    def prb_copy(h, slot, c, k):
        return to_wave(
            k,
            probe.at[slot, h, c, wav],
            probe.at[slot, h, c, wav],
            prb_ss.at[h, c, k],
            prb_rs.at[h, c, k],
        )

    def dot_copy(h, k):
        return to_section(k, dots_send.at[h], dots_recv.at[h, k], dot_ss.at[h, k], dot_rs.at[h, k])

    def stp_copy(h, k):
        return to_wave(k, steps.at[h, wav], steps.at[h, wav], stp_ss.at[h, k], stp_rs.at[h, k])

    def joined(blocks, width):
        return blocks.astype(f32).reshape(reals, width)

    def make_image(h, slot, arrive):
        for c in range(CHUNKS):
            arrive(c)
            lhs = joined(probe[slot, h, c], ac).astype(bf16)
            for j in range(CHUNKS):
                part = lax.dot_general(
                    lhs,
                    jac[j * rc:(j + 1) * rc, c * ac:(c + 1) * ac],
                    (((1,), (1,)), ((), ())),
                    preferred_element_type=f32,
                )
                if c:
                    part = acc[:, j * rc:(j + 1) * rc] + part
                if c < CHUNKS - 1:
                    acc[:, j * rc:(j + 1) * rc] = part
                else:
                    sec_part[h, j] = part.reshape(n, rb, rc).astype(bf16)
                    for k in peers:
                        sec_copy(h, j, k).start()

    def take_image(h, j):
        for k in peers:
            sec_copy(h, j, k).wait()
        total = sec_part[h, j, sec].astype(f32)
        for k in peers:
            total = total + sec_recv[h, j, k].astype(f32)
        return total

    def send_masked(h, j, values):
        masked[h, j, sec] = (weight_ref[:, j * rc:(j + 1) * rc] * values).astype(bf16)
        for k in peers:
            msk_copy(h, j, k).start()

    def make_back(h):
        for j in range(CHUNKS):
            for k in peers:
                msk_copy(h, j, k).wait()
            lhs = joined(masked[h, j], rc).astype(bf16)
            for c in range(CHUNKS):
                part = jnp.dot(
                    lhs,
                    jac[j * rc:(j + 1) * rc, c * ac:(c + 1) * ac],
                    preferred_element_type=f32,
                )
                if j:
                    part = acc[:, c * ac:(c + 1) * ac] + part
                if j < CHUNKS - 1:
                    acc[:, c * ac:(c + 1) * ac] = part
                else:
                    wav_part[h, c] = part.reshape(n, rb, ac).astype(bf16)
                    for k in peers:
                        wav_copy(h, c, k).start()

    def take_back(h, c):
        for k in peers:
            wav_copy(h, c, k).wait()
        total = wav_part[h, c, wav].astype(f32)
        for k in peers:
            total = total + wav_recv[h, c, k].astype(f32)
        return total

    lane = lax.broadcasted_iota(jnp.int32, (rb, LANES), 1)

    def send_dots(h, values):
        packed = jnp.zeros((rb, LANES), f32)
        for at, value in enumerate(values):
            packed = jnp.where(lane == at, value, packed)
        dots_send[h] = packed
        for k in peers:
            dot_copy(h, k).start()

    def take_dots(h, count):
        for k in peers:
            dot_copy(h, k).wait()
        total = dots_send[h]
        for k in peers:
            total = total + dots_recv[h, k]
        return [total[:, at:at + 1] for at in range(count)]

    def row_sum(values):
        return jnp.sum(values, axis=1, keepdims=True)

    def send_probe(h, slot, c, values):
        probe[slot, h, c, wav] = values.astype(bf16)
        for k in peers:
            prb_copy(h, slot, c, k).start()

    def take_steps(h, slot):
        for k in peers:
            stp_copy(h, k).wait()
        for j in range(CHUNKS):
            field[h, j] = field[h, j] + steps[h, sec][:, 0:1] * image[h, j]
        column = steps[h].reshape(reals, LANES)[:, 0:1]
        own = slice(h * reals, (h + 1) * reals)
        for c in range(CHUNKS):
            cols = slice(c * ac, (c + 1) * ac)
            cmd_ref[own, cols] = cmd_ref[own, cols] + column * joined(probe[slot, h, c], ac)

    cmd_ref[...] = start_ref[...]
    for h in streams:
        for c in range(CHUNKS):
            probe[0, h, c] = (
                start_ref[h * reals:(h + 1) * reals, c * ac:(c + 1) * ac]
                .reshape(n, rb, ac)
                .astype(bf16)
            )
    load.wait()
    for h in streams:
        make_image(h, 0, lambda c: None)
    for h in streams:
        for j in range(CHUNKS):
            field[h, j] = base_ref[h * rb:(h + 1) * rb, j * rc:(j + 1) * rc] + take_image(h, j)

    def iteration(_, carry):
        for h in streams:
            for j in range(CHUNKS):
                send_masked(h, j, field[h, j])
        for h in streams:
            make_back(h)
        for h in streams:
            square = jnp.zeros((rb, 1), f32)
            for c in range(CHUNKS):
                start = -take_back(h, c)
                residual[h, c] = start
                direction[h, c] = start
                send_probe(h, 0, c, start)
                square = square + row_sum(start * start)
            send_dots(h, [square])
        for h in streams:
            (first,) = take_dots(h, 1)
            norm[h] = jnp.broadcast_to(first, (rb, LANES))

        def cg_step(step, carry):
            slot = lax.rem(step, 2)

            for h in streams:

                def arrive(c):
                    for k in peers:
                        prb_copy(h, slot, c, k).wait()

                make_image(h, slot, arrive)

                @pl.when(step > 0)
                def _():
                    take_steps(h, 1 - slot)

            for h in streams:
                for j in range(CHUNKS):
                    total = take_image(h, j)
                    image[h, j] = total
                    send_masked(h, j, total)
            for h in streams:
                make_back(h)
            for h in streams:
                dd = jnp.zeros((rb, 1), f32)
                ra, aa = dd, dd
                for c in range(CHUNKS):
                    along = direction[h, c]
                    applied = take_back(h, c) + regul_ref[:, c * ac:(c + 1) * ac] * along
                    applied_ref[h, c] = applied
                    dd = dd + row_sum(along * applied)
                    ra = ra + row_sum(residual[h, c] * applied)
                    aa = aa + row_sum(applied * applied)
                send_dots(h, [dd, ra, aa])
            for h in streams:
                curvature, ra, aa = take_dots(h, 3)
                norm_now = norm[h][:, 0:1]
                step_len = norm_now / (curvature + epsilon)
                norm_next = jnp.maximum(norm_now + step_len * (step_len * aa - 2.0 * ra), 0.0)
                ratio = norm_next / (norm_now + epsilon)
                norm[h] = jnp.broadcast_to(norm_next, (rb, LANES))

                @pl.when(step < CG - 1)
                def _():
                    for c in range(CHUNKS):
                        after = residual[h, c] - step_len * applied_ref[h, c]
                        residual[h, c] = after
                        ahead = after + ratio * direction[h, c]
                        direction[h, c] = ahead
                        send_probe(h, 1 - slot, c, ahead)

                steps[h, wav] = jnp.broadcast_to(step_len, (rb, LANES))
                for k in peers:
                    stp_copy(h, k).start()

            return carry

        lax.fori_loop(0, CG, cg_step, 0)
        for h in streams:
            take_steps(h, (CG - 1) % 2)
        return carry

    lax.fori_loop(0, ITERS, iteration, 0)

    for h in streams:
        for j in range(CHUNKS):
            masked[h, j, sec] = field[h, j].astype(bf16)
            for k in peers:
                msk_copy(h, j, k).start()
    for h in streams:
        for j in range(CHUNKS):
            for k in peers:
                msk_copy(h, j, k).wait()
            out_ref[h * reals:(h + 1) * reals, j * rc:(j + 1) * rc] = joined(masked[h, j], rc)


def kernel_shards(nominal_field, sensitivity, aberrations, jacobian, tile_mask, regul, initial_commands):
    f32, bf16 = jnp.float32, jnp.bfloat16
    components, pixels, acts = jacobian.shape[1:]
    rows = components * pixels
    reals = initial_commands.shape[0]
    n = lax.axis_size("section")
    rb = reals // (n * STREAMS)
    rc, ac = rows // CHUNKS, acts // CHUNKS
    tile_count = tile_mask.shape[1]
    weight = jnp.broadcast_to(
        tile_mask[0].astype(f32)[None, :, None],
        (components, tile_count, pixels // tile_count),
    ).reshape(1, rows)
    own = lax.dynamic_index_in_dim(
        aberrations.reshape(STREAMS, n, rb, -1), lax.axis_index("section"), 1, keepdims=False
    ).reshape(STREAMS * rb, -1)
    base = nominal_field[0][None] + lax.dot_general(
        own, sensitivity[0], (((1,), (0,)), ((), ())), preferred_element_type=f32
    )
    vmem = pl.BlockSpec(memory_space=pltpu.VMEM)
    dma = pltpu.SemaphoreType.DMA
    commands, field = pl.pallas_call(
        functools.partial(control_kernel, n, rb),
        out_shape=(
            jax.ShapeDtypeStruct((reals, acts), f32),
            jax.ShapeDtypeStruct((reals, rows), f32),
        ),
        in_specs=[pl.BlockSpec(memory_space=pl.ANY), vmem, vmem, vmem, vmem],
        out_specs=(vmem, vmem),
        scratch_shapes=[
            pltpu.VMEM((rows, acts), bf16),
            pltpu.VMEM((2, STREAMS, CHUNKS, n, rb, ac), bf16),
            pltpu.VMEM((STREAMS, CHUNKS, n, rb, rc), bf16),
            pltpu.VMEM((STREAMS, CHUNKS, n, rb, rc), bf16),
            pltpu.VMEM((STREAMS, CHUNKS, n - 1, rb, rc), bf16),
            pltpu.VMEM((STREAMS, CHUNKS, n, rb, ac), bf16),
            pltpu.VMEM((STREAMS, CHUNKS, n - 1, rb, ac), bf16),
            pltpu.VMEM((STREAMS, CHUNKS, rb, rc), f32),
            pltpu.VMEM((STREAMS, CHUNKS, rb, rc), f32),
            pltpu.VMEM((STREAMS, CHUNKS, rb, ac), f32),
            pltpu.VMEM((STREAMS, CHUNKS, rb, ac), f32),
            pltpu.VMEM((n * rb, max(rows, acts)), f32),
            pltpu.VMEM((STREAMS, CHUNKS, rb, ac), f32),
            pltpu.VMEM((STREAMS, rb, LANES), f32),
            pltpu.VMEM((STREAMS, n - 1, rb, LANES), f32),
            pltpu.VMEM((STREAMS, rb, LANES), f32),
            pltpu.VMEM((STREAMS, n, rb, LANES), f32),
            dma(()),
        ]
        + [dma((STREAMS, CHUNKS, n - 1))] * 8
        + [dma((STREAMS, n - 1))] * 4,
        compiler_params=pltpu.CompilerParams(
            collective_id=0, has_side_effects=True, vmem_limit_bytes=40 * 1024 * 1024
        ),
        name="control_loop",
    )(
        jacobian.reshape(rows, acts),
        base.reshape(STREAMS * rb, rows),
        initial_commands,
        regul[None, :],
        weight,
    )
    return commands, field.reshape(reals, 1, components, pixels)


def solution(mesh):
    placed = (
        P("wave", None, None),
        P("wave", None, None, None),
        P("groups", None),
        P("wave", None, None, "section"),
        P("wave", None),
        P("section"),
        P("groups", "section"),
    )

    def choose(*args):
        n, waves = mesh.shape["section"], mesh.shape["wave"]
        reals = args[6].shape[0]
        acts = args[3].shape[3]
        rows = args[3].shape[1] * args[3].shape[2]
        fits = (
            n == waves
            and n > 1
            and reals % (8 * STREAMS * n) == 0
            and acts % (LANES * CHUNKS) == 0
            and rows % (LANES * CHUNKS) == 0
            and rows * acts <= 2048 * 2048
            and reals <= 64
        )
        return (kernel_shards if fits else general_shards)(*args)

    return jax.shard_map(
        choose,
        mesh=mesh,
        in_specs=placed,
        out_specs=(P("groups", "section"), P("groups", "wave", None, None)),
        check_vma=False,
    )
```

time: 327 us -> 295 us (0.902)
  Pallas kernels: 317 us -> 286 us
    pallas_call x1, Pallas kernels: 317 us -> 286 us  [kernel_shards(): pl.pallas_call(functools.partial(control_kernel, n, rb), out_shape=(jax.S...]
where the time goes in v2:
time: 295 us
  Pallas kernels  286 us (97%)
  local copies, waits for them, and re-layouts  6.84 us (2%)
    pallas_call x1, Pallas kernels, kernel_shards(): pl.pallas_call(functools.partial(control_kernel, n, rb), out_shape=(jax.S...  286 us

profile of v2, /device:TPU:0, one launch (start us, length us, event | category | flops | bytes accessed | tf_op | source)
XLA Modules:
  0.0 295.1 jit_solution(10225883616610268790)
XLA Ops:
  0.6 0.0 copy-start
  0.6 0.0 copy-start.2
  0.7 0.0 copy-start.3
  0.7 1.3 copy-done
  2.0 0.7 convert_bitcast_fusion
  2.7 0.1 broadcast_in_dim.10
  2.7 1.2 fusion.5
  4.0 0.0 copy-done.2
  4.0 0.0 copy-done.3
  4.0 0.0 copy-start.1
  4.0 3.4 %copy-done.1 = bf16[1,2,1024,2048]{3,2,1,0:T(8,128)(2,1)S(1)} copy-done((bf16[1,2,1024,2048]{3,2,1,0:T(8,128)(2,1)S(1)}, bf16[1,2,1024,2048]{3,2,1,0:T(8,128)(2,1)}, u32[]{:S(2)}) %copy-start.1) | copy-done | bytes 8388632
  7.4 285.7 %control_loop.1 = (f32[64,2048]{1,0:T(8,128)S(1)}, f32[64,2048]{1,0:T(8,128)S(1)}) custom-call(bf16[2048,2048]{1,0:T(8,128)(2,1)S(1)} %bitcast.20, f32[16,2048]{1,0:T(8,128)S(1)} %bitcast.21, f32[64,2048]{1,0:T(8,128)S(1)} %copy-done.2, f32[1,2048]{1,0:T(1,128)S(1)} %bitcast.23, f32[1,2048]{1,0:T(1,128)S(1)} %bitcast.22), custom_call_target="tpu_custom_call" | custom-call | tf_op jit(solution)/shard_map/control_loop/pallas_call | solution.py:431
  293.1 1.2 reshape.34
  294.3 0.8 copy.22
  (1 shorter events, 0.0 us)
Async XLA Ops:
  0.6 1.4 copy-start
  0.6 3.3 %copy-start.2 = (f32[64,2048]{1,0:T(8,128)S(1)}, f32[64,2048]{1,0:T(8,128)}, u32[]{:S(2)}) copy-start(f32[64,2048]{1,0:T(8,128)} %start_ref.1) | copy-start | bytes 1572868
  0.7 3.3 %copy-start.3 = (f32[2048]{0:T(1024)S(1)}, f32[2048]{0:T(1024)}, u32[]{:S(2)}) copy-start(f32[2048]{0:T(1024)} %param.12) | copy-start | bytes 24580
  4.0 3.4 %copy-start.1 = (bf16[1,2,1024,2048]{3,2,1,0:T(8,128)(2,1)S(1)}, bf16[1,2,1024,2048]{3,2,1,0:T(8,128)(2,1)}, u32[]{:S(2)}) copy-start(bf16[1,2,1024,2048]{3,2,1,0:T(8,128)(2,1)} %param.10) | copy-start | bytes 25165828

commit v3 on v2

--- a/solution.py
+++ b/solution.py
@@ -343,8 +343,9 @@
 
                 make_image(h, slot, arrive)
 
-                @pl.when(step > 0)
-                def _():
+            @pl.when(step > 0)
+            def _():
+                for h in streams:
                     take_steps(h, 1 - slot)
 
             for h in streams:

time: 295 us -> 294 us (level)
  no operation moved by 1% of the time
where the time goes in v3:
time: 294 us
  Pallas kernels  285 us (97%)
  local copies, waits for them, and re-layouts  6.84 us (2%)
    pallas_call x1, Pallas kernels, kernel_shards(): pl.pallas_call(functools.partial(control_kernel, n, rb), out_shape=(jax.S...  285 us

profile of v3, /device:TPU:0, one launch (start us, length us, event | category | flops | bytes accessed | tf_op | source)
XLA Modules:
  0.0 294.1 jit_solution(8495962342468741952)
XLA Ops:
  0.6 0.0 copy-start
  0.6 0.0 copy-start.2
  0.7 0.0 copy-start.3
  0.7 1.3 copy-done
  2.0 0.7 convert_bitcast_fusion
  2.7 0.1 broadcast_in_dim.10
  2.7 1.2 fusion.5
  4.0 0.0 copy-done.2
  4.0 0.0 copy-done.3
  4.0 0.0 copy-start.1
  4.0 3.4 %copy-done.1 = bf16[1,2,1024,2048]{3,2,1,0:T(8,128)(2,1)S(1)} copy-done((bf16[1,2,1024,2048]{3,2,1,0:T(8,128)(2,1)S(1)}, bf16[1,2,1024,2048]{3,2,1,0:T(8,128)(2,1)}, u32[]{:S(2)}) %copy-start.1) | copy-done | bytes 8388632
  7.4 284.7 %control_loop.1 = (f32[64,2048]{1,0:T(8,128)S(1)}, f32[64,2048]{1,0:T(8,128)S(1)}) custom-call(bf16[2048,2048]{1,0:T(8,128)(2,1)S(1)} %bitcast.20, f32[16,2048]{1,0:T(8,128)S(1)} %bitcast.21, f32[64,2048]{1,0:T(8,128)S(1)} %copy-done.2, f32[1,2048]{1,0:T(1,128)S(1)} %bitcast.23, f32[1,2048]{1,0:T(1,128)S(1)} %bitcast.22), custom_call_target="tpu_custom_call" | custom-call | tf_op jit(solution)/shard_map/control_loop/pallas_call | solution.py:432
  292.1 1.2 reshape.34
  293.4 0.8 copy.22
  (1 shorter events, 0.0 us)
Async XLA Ops:
  0.6 1.4 copy-start
  0.6 3.3 %copy-start.2 = (f32[64,2048]{1,0:T(8,128)S(1)}, f32[64,2048]{1,0:T(8,128)}, u32[]{:S(2)}) copy-start(f32[64,2048]{1,0:T(8,128)} %start_ref.1) | copy-start | bytes 1572868
  0.7 3.3 %copy-start.3 = (f32[2048]{0:T(1024)S(1)}, f32[2048]{0:T(1024)}, u32[]{:S(2)}) copy-start(f32[2048]{0:T(1024)} %param.12) | copy-start | bytes 24580
  4.0 3.4 %copy-start.1 = (bf16[1,2,1024,2048]{3,2,1,0:T(8,128)(2,1)S(1)}, bf16[1,2,1024,2048]{3,2,1,0:T(8,128)(2,1)}, u32[]{:S(2)}) copy-start(bf16[1,2,1024,2048]{3,2,1,0:T(8,128)(2,1)} %param.10) | copy-start | bytes 25165828
